TPU v7x, 128 devices: a whole 4x4x4 slice. The times are simulated.
128 devices in a mesh: dp: 128 (over z, x, y, core).
Axes of the slice: x: 4, y: 4, z: 4, core: 2. Of those that a mesh axis runs over, the one named last changes fastest.
Arguments:
- hidden: bfloat16 [256, 512, 2048], P('dp'), may hold values from -6 to 6
- lengths: int32 [256], P('dp'), may hold values from 1 to 512, 65536 in all
- order: int32 [256], P('dp'), may hold values from 0 to 255, each once
- candidates: int32 [256, 64], replicated, may hold values from 0 to 65535, as said below
- norm_gain: float32 [2048], replicated, may hold values from 0.25 to 1.75
- w_query: bfloat16 [2048, 1024], P('dp'), may hold values from -1 to 1
- w_key: bfloat16 [2048, 1024], P('dp'), may hold values from -1 to 1
- w_value: bfloat16 [2048, 1024], P('dp'), may hold values from -0.125 to 0.125
- w_out: bfloat16 [1024, 2048], P('dp'), may hold values from -0.75 to 0.75
- index_rows: bfloat16 [65536, 2048], P('dp'), may hold values from -0.125 to 0.125
Outputs:
- scores: float32 [256, 64], P('dp')
Inputs may be any that keep to these rules, and one draw needn't show every extreme that they name: The candidates of many texts may all lie in the index rows of one device: in every draw at least half of the texts have all 64 of their candidates in the 512 index rows of one device, the same device for all of them.
All inputs are finite; a program needn't handle non-finite values. No bound on the sum of `lengths` on one device may be relied on, other than what follows from the above.
Results may differ from a plain program's by a relative error of at most 0.005.
Values may be sent and summed in bfloat16 or wider, within the bound.
No kernel may reach another device: no remote copies, remote signals or barrier semaphores. Data moves between devices by JAX's collectives and lax.ppermute only.
A program may use at most 128 MiB of HBM per device.

v0:
```python
import jax
import jax.numpy as jnp
from jax import lax
from jax.sharding import PartitionSpec as P

HEAD = 64


def attend_text(bundle):
    queries, key_side, value_side, length = bundle
    slots = queries.shape[0]
    logits = jnp.einsum("qhd,khd->hqk", queries, key_side, preferred_element_type=jnp.float32)
    valid = jnp.arange(slots, dtype=jnp.int32) < length
    logits = jnp.where(valid[None, None, :], logits, jnp.float32(-1e30))
    probs = jax.nn.softmax(logits, axis=-1).astype(jnp.bfloat16)
    context = jnp.einsum("hqk,khd->qhd", probs, value_side, preferred_element_type=jnp.float32)
    return context.astype(jnp.bfloat16)


def per_device(
    hidden, lengths, order, candidates, norm_gain, w_query, w_key, w_value, w_out, index_rows
):
    texts, lmax, width = hidden.shape
    slots = texts * lmax
    features = w_query.shape[1]
    heads = features // HEAD
    flat = hidden.reshape(slots, width)
    values_f = flat.astype(jnp.float32)
    meansq = jnp.mean(values_f * values_f, axis=-1, keepdims=True)
    normed = (values_f * lax.rsqrt(meansq + 1e-06) * norm_gain).astype(jnp.bfloat16)
    full_query, full_key, full_value = (
        lax.all_gather(w_query, "dp", axis=0, tiled=True),
        lax.all_gather(w_key, "dp", axis=0, tiled=True),
        lax.all_gather(w_value, "dp", axis=0, tiled=True),
    )
    query_sum = jnp.dot(normed, full_query, preferred_element_type=jnp.float32)
    key_sum = jnp.dot(normed, full_key, preferred_element_type=jnp.float32)
    value_sum = jnp.dot(normed, full_value, preferred_element_type=jnp.float32)
    queries = query_sum.astype(jnp.bfloat16).reshape(texts, lmax, heads, HEAD)
    key_side = key_sum.astype(jnp.bfloat16).reshape(texts, lmax, heads, HEAD)
    value_side = value_sum.astype(jnp.bfloat16).reshape(texts, lmax, heads, HEAD)
    context = lax.map(attend_text, (queries, key_side, value_side, lengths)).reshape(
        slots, features
    )
    projected = jnp.dot(
        context, lax.all_gather(w_out, "dp", axis=0, tiled=True), preferred_element_type=jnp.float32
    )
    layer_out = (values_f + projected).reshape(texts, lmax, width)
    valid = jnp.arange(lmax, dtype=jnp.int32)[None, :] < lengths[:, None]
    pooled = (
        jnp.sum(jnp.where(valid[:, :, None], layer_out, jnp.float32(0.0)), axis=1)
        / lengths.astype(jnp.float32)[:, None]
    )
    unit = (pooled * lax.rsqrt(jnp.mean(pooled * pooled, axis=-1, keepdims=True) + 1e-06)).astype(
        jnp.bfloat16
    )
    order_all = lax.all_gather(order, "dp", axis=0, tiled=True)
    cand_proc = candidates[order_all]
    rows_dev = index_rows.shape[0]
    device = lax.axis_index("dp")
    local_scores = lax.dot_general(
        lax.all_gather(unit, "dp", axis=0, tiled=True),
        index_rows,
        (((1,), (1,)), ((), ())),
        preferred_element_type=jnp.float32,
    )
    owner = cand_proc // rows_dev
    within = cand_proc - owner * rows_dev
    picked = jnp.take_along_axis(local_scores, jnp.clip(within, 0, rows_dev - 1), axis=1)
    partial_value = jnp.where(owner == device, picked, jnp.float32(0.0))
    inverse = jnp.argsort(order_all)
    mine = lax.psum_scatter(partial_value, "dp", scatter_dimension=0, tiled=True)
    every_score = lax.all_gather(mine, "dp", axis=0, tiled=True)
    wanted_rows = lax.dynamic_slice_in_dim(inverse, device * texts, texts, 0)
    return every_score[wanted_rows]


def solution(mesh):
    return jax.shard_map(
        per_device,
        mesh=mesh,
        in_specs=(
            P("dp", None, None),
            P("dp"),
            P("dp"),
            P(),
            P(),
            P("dp", None),
            P("dp", None),
            P("dp", None),
            P("dp", None),
            P("dp", None),
        ),
        out_specs=P("dp", None),
        check_vma=False,
    )
```

profile of v0, /device:TPU:1, one launch (start us, length us, event | category | flops | bytes accessed | tf_op | source)
XLA Modules:
  0.0 678.7 jit_solution(16129564787788719315)
XLA Ops:
  6.5 0.0 copy-start
  6.5 0.0 all-gather.8.cloned.1.call-start
  6.5 0.7 all-gather.8.cloned.1.call-update
  7.3 0.0 all-gather.10.cloned.1.call-start
  7.3 0.7 all-gather.10.cloned.1.call-update
  8.0 0.0 all-gather.12.cloned.1.call-start
  8.1 0.7 all-gather.12.cloned.1.call-update
  8.7 0.0 all-gather.14.cloned.1.call-start
  8.8 0.5 all-gather.14.cloned.1.call-update
  9.3 0.0 all-gather.16.cloned.1.call-start
  9.4 1.3 iota_compare_fusion.1
  10.7 1.2 convert_element_type.43
  11.9 3.1 fusion.39
  15.0 0.0 copy-done.2
  15.0 5.2 fusion.41
  20.2 60.4 %all-gather.8.cloned.1.call-done = bf16[2048,1024]{1,0:T(8,128)(2,1)} async-done(((bf16[16,1024]{1,0:T(8,128)(2,1)}), bf16[2048,1024]{1,0:T(8,128)(2,1)}) %all-gather.8.cloned.1.call-update) | async-done | bytes 4194320 | tf_op jit(solution)/shard_map/all_gather | solution.py:34
  80.6 9.3 %convolution_convert_fusion.2 = bf16[1024,1024]{1,0:T(8,128)(2,1)} fusion(bf16[1024,2048]{1,0:T(8,128)(2,1)} %fusion.41, bf16[2048,1024]{1,0:T(8,128)(2,1)} %all-gather.8.cloned.1.call-done), kind=kOutput, calls=%fused_computation.40 | convolution fusion | flops 4296015872 | bytes 10485760 | tf_op jit(solution)/shard_map/dot_general | solution.py:38
  89.8 6.4 reshape.182
  96.3 5.5 copy.30
  101.7 46.1 %all-gather.10.cloned.1.call-done = bf16[2048,1024]{1,0:T(8,128)(2,1)} async-done(((bf16[16,1024]{1,0:T(8,128)(2,1)}), bf16[2048,1024]{1,0:T(8,128)(2,1)}) %all-gather.10.cloned.1.call-update) | async-done | bytes 4194320 | tf_op jit(solution)/shard_map/all_gather | solution.py:32
  147.8 9.3 %convolution_convert_fusion.1 = bf16[1024,1024]{1,0:T(8,128)(2,1)} fusion(bf16[1024,2048]{1,0:T(8,128)(2,1)} %fusion.41, bf16[2048,1024]{1,0:T(8,128)(2,1)} %all-gather.10.cloned.1.call-done), kind=kOutput, calls=%fused_computation.39 | convolution fusion | flops 4296015872 | bytes 10485760 | tf_op jit(solution)/shard_map/dot_general | solution.py:36
  157.1 6.4 reshape.183
  163.6 5.4 copy.31
  169.0 46.2 %all-gather.12.cloned.1.call-done = bf16[2048,1024]{1,0:T(8,128)(2,1)} async-done(((bf16[16,1024]{1,0:T(8,128)(2,1)}), bf16[2048,1024]{1,0:T(8,128)(2,1)}) %all-gather.12.cloned.1.call-update) | async-done | bytes 4194320 | tf_op jit(solution)/shard_map/all_gather | solution.py:33
  215.2 9.3 %convolution_convert_fusion = bf16[1024,1024]{1,0:T(8,128)(2,1)} fusion(bf16[1024,2048]{1,0:T(8,128)(2,1)} %fusion.41, bf16[2048,1024]{1,0:T(8,128)(2,1)} %all-gather.12.cloned.1.call-done), kind=kOutput, calls=%fused_computation.38 | convolution fusion | flops 4296015872 | bytes 10485760 | tf_op jit(solution)/shard_map/dot_general | solution.py:37
  224.5 6.4 reshape.184
  230.9 5.5 copy.32
  236.4 42.3 %while.10 = (s32[]{:T(128)}, bf16[2,512,16,64]{1,3,2,0:T(8,128)(2,1)}, bf16[2,512,16,64]{1,3,2,0:T(8,128)(2,1)}, s32[2]{0:T(128)S(1)}, bf16[2,512,16,64]{1,3,2,0...) while((s32[]{:T(128)}, bf16[2,512,16,64]{1,3,2,0:T(8,128)(2,1)}, ...), condition=%wide.region_4.5_spmd, body=%wide.region_1.4_spmd.sunk | while | flops 1095238656 | bytes 37817436 | solution.py:42
  236.4 0.7 dynamic_slice.62
  237.0 0.7 iota_compare_fusion.3
  237.7 10.8 %fusion.82 = (f32[16,512]{1,0:T(8,128)S(1)}, f32[16,512,512]{1,2,0:T(8,128)}) fusion(pred[512]{0:T(512)(128)(4,1)S(1)} %iota_compare_fusion.3, bf16[2,512,16,64]{1,3,2,0:T(8,128)(2,1)} %get-tuple-element.134, s32[]{:T(128)} %get-tuple-element.122, bf16[2,512,16,64]{1,3,2,0:T(8,128)(2,1)} %get-tuple-element.133), kind=kOutput, calls=%fused_computation.78.clone.1 | convolution fusion | flops 549454336 | bytes 18908672 | tf_op jit(solution)/shard_map/while/body/eval_jaxpr/sub | solution.py:15
  248.5 8.8 %fusion.83 = bf16[2,512,16,64]{1,3,2,0:T(8,128)(2,1)} fusion(bf16[2,512,16,64]{1,3,2,0:T(8,128)(2,1)} %get-tuple-element.123, s32[]{:T(128)} %get-tuple-element.122, f32[16,512,512]{1,2,0:T(8,128)} %get-tuple-element.113, f32[16,512]{1,0:T(8,128)S(1)} %get-tuple-element.114, bf16[2,512,16,64]{1,3,2,0:T(8,128)(2,1)} %get-tuple-element.131), kind=kOutput, calls=%fused_computation.14.clone.1 | convolution fusion | flops 545783808 | bytes 18908160 | tf_op jit(solution)/shard_map/while/body/eval_jaxpr/hqk,khd->qhd/dot_general | solution.py:16
  257.3 0.7 dynamic_slice.62
  257.9 0.7 iota_compare_fusion.3
  258.6 10.8 %fusion.82 = (f32[16,512]{1,0:T(8,128)S(1)}, f32[16,512,512]{1,2,0:T(8,128)}) fusion(pred[512]{0:T(512)(128)(4,1)S(1)} %iota_compare_fusion.3, bf16[2,512,16,64]{1,3,2,0:T(8,128)(2,1)} %get-tuple-element.134, s32[]{:T(128)} %get-tuple-element.122, bf16[2,512,16,64]{1,3,2,0:T(8,128)(2,1)} %get-tuple-element.133), kind=kOutput, calls=%fused_computation.78.clone.1 | convolution fusion | flops 549454336 | bytes 18908672 | tf_op jit(solution)/shard_map/while/body/eval_jaxpr/sub | solution.py:15
  269.4 9.2 %fusion.83 = bf16[2,512,16,64]{1,3,2,0:T(8,128)(2,1)} fusion(bf16[2,512,16,64]{1,3,2,0:T(8,128)(2,1)} %get-tuple-element.123, s32[]{:T(128)} %get-tuple-element.122, f32[16,512,512]{1,2,0:T(8,128)} %get-tuple-element.113, f32[16,512]{1,0:T(8,128)S(1)} %get-tuple-element.114, bf16[2,512,16,64]{1,3,2,0:T(8,128)(2,1)} %get-tuple-element.131), kind=kOutput, calls=%fused_computation.14.clone.1 | convolution fusion | flops 545783808 | bytes 18908160 | tf_op jit(solution)/shard_map/while/body/eval_jaxpr/hqk,khd->qhd/dot_general | solution.py:16
  278.6 3.8 copy.33
  282.4 1.9 copy.42
  284.4 0.0 copy-done.3
  284.4 0.0 copy-start.6
  284.4 9.2 %select_reduce_fusion.1 = f32[2,2048]{1,0:T(2,128)S(1)} fusion(pred[2,512]{1,0:T(4,128)(4,1)S(1)} %copy-done.3, bf16[1024,1024]{0,1:T(8,128)(2,1)} %bitcast.100, bf16[1024,2048]{1,0:T(8,128)(2,1)} %all-gather.14.cloned.1.call-done, bf16[2,512,2048]{2,1,0:T(8,128)(2,1)} %param.12), kind=kOutput, calls=%fused_computation.37 | convolution fusion | flops 4303351808 | bytes 10503168 | tf_op jit(solution)/shard_map/dot_general | solution.py:45
  293.6 0.2 multiply_reduce_fusion
  293.9 0.7 fusion.53
  294.5 0.0 all-gather.16.cloned.1.call-update
  294.6 0.0 all-reduce.4.cloned.1.call-start
  294.6 0.0 copy-done.1
  294.6 0.1 copy.26
  294.7 0.2 dynamic-update-slice
  295.0 63.0 %all-reduce = s32[256]{0:T(256)S(1)} all-reduce(s32[256]{0:T(256)S(1)} %dynamic-update-slice), channel_id=1, replica_groups=mesh['dp'=128] {'dp'}, use_global_device_ids=true, to_apply=%add | all-reduce | flops 256 | bytes 2048
  358.0 0.7 gather_fusion
  358.8 0.1 fusion.49
  358.9 0.1 reshape.168
  359.0 3.2 sort.17
  362.2 0.1 compare_select_fusion.3
  362.3 2.3 reshape.179
  364.5 2.0 fusion.63
  366.5 129.5 %gather_fusion.2 = f32[16384]{0:T(1024)S(1)} fusion(f32[256,512]{1,0:T(8,128)S(1)} %fusion.63, s32[16384]{0:T(1024)S(1)} %reshape.168), kind=kCustom, calls=%fused_computation.2 | custom fusion | bytes 262144 | tf_op jit(solution)/shard_map/jit(take_along_axis)/gather | solution.py:69
  496.0 0.1 reshape.171
  496.1 0.8 select_select_fusion
  496.9 0.0 all-reduce.4.cloned.1.call-update
  496.9 139.4 %all-reduce.4.cloned.1.call-done = f32[256,64]{1,0:T(8,128)} async-done(((f32[256,64]{1,0:T(8,128)}), f32[256,64]{1,0:T(8,128)}) %all-reduce.4.cloned.1.call-update) | async-done | bytes 65552
  636.3 0.7 dynamic-slice_bitcast_fusion
  637.0 33.8 %all-gather.1 = f32[128,2,64]{2,1,0:T(2,128)S(1)} all-gather(f32[1,2,64]{2,1,0:T(2,128)S(1)} %dynamic-slice_bitcast_fusion), channel_id=1, replica_groups=mesh['dp'=128] {'dp'}, dimensions={0}, use_global_device_ids=true | all-gather | bytes 66048 | tf_op jit(solution)/shard_map/all_gather | solution.py:73
  670.8 1.1 gather_fusion.1
  (20 shorter events, 0.1 us)
Async XLA Ops:
  6.5 358.0 %copy-start = (bf16[512,2048]{1,0:T(8,128)(2,1)S(1)}, bf16[512,2048]{1,0:T(8,128)(2,1)}, u32[]{:S(2)}) copy-start(bf16[512,2048]{1,0:T(8,128)(2,1)} %param.21) | copy-start | bytes 6291460
  6.5 8.5 %copy-start.2 = (f32[2048]{0:T(1024)S(1)}, f32[2048]{0:T(1024)}, u32[]{:S(2)}) copy-start(f32[2048]{0:T(1024)} %param.16) | copy-start | bytes 24580
  6.5 74.0 %all-gather.8.cloned.1.call-start = ((), (), s32[]{:S(2)}) async-start(), calls=%async_computation | async-start | bytes 4227072 | tf_op jit(solution)/shard_map/all_gather | solution.py:34
  7.3 140.6 %all-gather.10.cloned.1.call-start = ((), (), s32[]{:S(2)}) async-start(), calls=%async_computation.1 | async-start | bytes 4227072 | tf_op jit(solution)/shard_map/all_gather | solution.py:32
  8.0 207.2 %all-gather.12.cloned.1.call-start = ((), (), s32[]{:S(2)}) async-start(), calls=%async_computation.2 | async-start | bytes 4227072 | tf_op jit(solution)/shard_map/all_gather | solution.py:33
  8.7 275.6 %all-gather.14.cloned.1.call-start = ((), (), s32[]{:S(2)}) async-start(), calls=%async_computation.3 | async-start | bytes 4227072 | tf_op jit(solution)/shard_map/all_gather | solution.py:46
  9.3 352.9 %all-gather.16.cloned.1.call-start = ((), (), s32[]{:S(2)}) async-start(), calls=%async_computation.4 | async-start | bytes 1056768 | tf_op jit(solution)/shard_map/all_gather | solution.py:62
  230.9 5.5 copy-start.5
  278.6 5.7 copy-start.3
  284.4 9.3 %copy-start.4 = (f32[2]{0:T(128)S(1)}, f32[2]{0:T(128)}, u32[]{:S(2)}) copy-start(f32[2]{0:T(128)} %convert_element_type.43) | copy-start | bytes 28
  284.4 10.2 %copy-start.1 = (s32[256,64]{0,1:T(8,128)S(1)}, s32[256,64]{0,1:T(8,128)}, u32[]{:S(2)}) copy-start(s32[256,64]{0,1:T(8,128)} %param.15) | copy-start | bytes 196612
  284.4 10.4 %copy-start.6 = (s32[2]{0:T(128)S(1)}, s32[2]{0:T(128)}, u32[]{:S(2)}) copy-start(s32[2]{0:T(128)} %param.14) | copy-start | bytes 28
  294.6 341.8 %all-reduce.4.cloned.1.call-start = ((), (), s32[]{:S(2)}) async-start(), calls=%async_computation.5 | async-start | bytes 262144
Sparse Core Ops, SparseCore 0:
  10.5 70.0 all-gather.7
  83.7 64.1 all-gather.9
  151.0 64.1 all-gather.11
  218.1 64.1 all-gather.13
  294.7 61.1 all-gather.15
  497.0 139.2 all-reduce.3
where the time goes:
time: 680 us; the launch traced here: 679 us
  waiting for transfers between devices  295 us (43%)
  local copies, waits for them, and re-layouts  177 us (26%)
  blocking collectives  96.8 us (14%)
  matrix products  78.7 us (12%)
  other arithmetic  17.3 us (3%)
  between operations  13.6 us (2%)
    unnamed x7, waiting for transfers between devices  142 us
    gather x3, local copies, waits for them, and re-layouts, per_device(): jnp.take_along_axis(local_scores, jnp.clip(within, 0, rows_dev - 1), axis=1)  130 us
    unnamed x1, blocking collectives  63 us
    all_gather x1, waiting for transfers between devices, per_device(): lax.all_gather(w_value, 'dp', axis=0, tiled=True)  60.4 us
    all_gather x1, waiting for transfers between devices, per_device(): lax.all_gather(w_key, 'dp', axis=0, tiled=True)  46.2 us
    all_gather x1, waiting for transfers between devices, per_device(): lax.all_gather(w_query, 'dp', axis=0, tiled=True)  46.1 us
    all_gather x1, blocking collectives, per_device(): every_score = lax.all_gather(mine, 'dp', axis=0, tiled=True)  33.8 us
    sub x2, matrix products, attend_text(): probs = jax.nn.softmax(logits, axis=-1).astype(jnp.bfloat16)  21.5 us
  transfers between devices with their start and end apart: 6, of which 4 were waited for; matrix products, arithmetic and copies ran while one was open for 19% of the time, Pallas kernels for 0%

commit v1 on v0

--- a/solution.py
+++ b/solution.py
@@ -29,7 +29,9 @@
     meansq = jnp.mean(values_f * values_f, axis=-1, keepdims=True)
     normed = (values_f * lax.rsqrt(meansq + 1e-06) * norm_gain).astype(jnp.bfloat16)
     full_query, full_key, full_value = (
-        lax.all_gather(w_query, "dp", axis=0, tiled=True),
+        jnp.concatenate(
+            lax.all_to_all(jnp.stack([w_query] * lax.axis_size("dp")), "dp", 0, 0), axis=0
+        ),
         lax.all_gather(w_key, "dp", axis=0, tiled=True),
         lax.all_gather(w_value, "dp", axis=0, tiled=True),
     )

time: 680 us -> 638 us (0.938)
  waiting for transfers between devices: 295 us -> 236 us
  starting transfers between devices: 0.2 us -> 12.1 us
    all_gather x1, waiting for transfers between devices: 60.4 us -> 9.19 us  [per_device(): lax.all_gather(w_value, 'dp', axis=0, tiled=True)]
    all_gather x1 -> x0, waiting for transfers between devices: 46.1 us -> none  [per_device(): lax.all_gather(w_query, 'dp', axis=0, tiled=True)]
    all_to_all x0 -> x1, waiting for transfers between devices: none -> 39.5 us  [per_device(): lax.all_to_all(jnp.stack([w_query] * lax.axis_size('dp')), 'dp', 0, 0)]
    all_to_all x0 -> x1, starting transfers between devices: none -> 11.9 us  [per_device(): lax.all_to_all(jnp.stack([w_query] * lax.axis_size('dp')), 'dp', 0, 0)]
    unnamed x7 -> x6, waiting for transfers between devices: 142 us -> 142 us
  transfers between devices with their start and end apart: 6 -> 6, of which waited for: 4 -> 4; matrix products, arithmetic and copies ran while one was open for 19% -> 21% of each run, Pallas kernels for 0% -> 0%
where the time goes in v1:
time: 638 us; the launch traced here: 637 us
  waiting for transfers between devices  236 us (37%)
  local copies, waits for them, and re-layouts  181 us (28%)
  blocking collectives  96.8 us (15%)
  matrix products  78.6 us (12%)
  other arithmetic  19.1 us (3%)
  between operations  13.3 us (2%)
  starting transfers between devices  12.1 us (2%)
    unnamed x6, waiting for transfers between devices  142 us
    gather x3, local copies, waits for them, and re-layouts, per_device(): jnp.take_along_axis(local_scores, jnp.clip(within, 0, rows_dev - 1), axis=1)  130 us
    unnamed x1, blocking collectives  63 us
    all_gather x1, waiting for transfers between devices, per_device(): lax.all_gather(w_key, 'dp', axis=0, tiled=True)  46 us
    all_to_all x1, waiting for transfers between devices, per_device(): lax.all_to_all(jnp.stack([w_query] * lax.axis_size('dp')), 'dp', 0, 0)  39.5 us
    all_gather x1, blocking collectives, per_device(): every_score = lax.all_gather(mine, 'dp', axis=0, tiled=True)  33.8 us
    sub x2, matrix products, attend_text(): probs = jax.nn.softmax(logits, axis=-1).astype(jnp.bfloat16)  21.6 us
    while x4, local copies, waits for them, and re-layouts, per_device(): lax.map(attend_text, (queries, key_side, value_side, lengths))  20.3 us
  transfers between devices with their start and end apart: 6, of which 4 were waited for; matrix products, arithmetic and copies ran while one was open for 21% of the time, Pallas kernels for 0%

profile of v1, /device:TPU:1, one launch (start us, length us, event | category | flops | bytes accessed | tf_op | source)
XLA Modules:
  0.0 637.1 jit_solution(1819468844518484282)
XLA Ops:
  6.5 0.0 copy-start
  6.5 0.7 all-gather.7.cloned.1.call-update
  7.3 0.0 all-gather.9.cloned.1.call-start
  7.3 0.7 all-gather.9.cloned.1.call-update
  8.0 3.3 stack.2
  11.3 11.9 %all-to-all-start = ((bf16[128,16,1024]{2,1,0:T(8,128)(2,1)}), bf16[128,16,1024]{2,1,0:T(8,128)(2,1)}, u32[]{:S(2)}, u32[]{:S(2)}) async-start(bf16[128,16,1024]{2,1,0:T(8,128)(2,1)} %stack.2), calls=%async_computation | async-start | bytes 8388608 | tf_op jit(solution)/shard_map/all_to_all | solution.py:33
  23.2 0.0 copy-start.6
  23.2 0.0 copy-start.3
  23.2 0.0 all-gather.11.cloned.1.call-start
  23.3 0.7 all-gather.11.cloned.1.call-update
  24.0 0.0 all-gather.13.cloned.1.call-start
  24.0 3.1 fusion.39
  27.2 0.6 convert_element_type.51
  27.8 0.7 iota_compare_fusion.1
  28.4 5.3 fusion.43
  33.7 3.0 fusion.41
  36.7 39.5 %all-to-all-done = bf16[128,16,1024]{2,1,0:T(8,128)(2,1)} async-done(((bf16[128,16,1024]{2,1,0:T(8,128)(2,1)}), bf16[128,16,1024]{2,1,0:T(8,128)(2,1)}, u32[]{:S(2)}, u32[]{:S(2)}) %all-to-all-start) | async-done | bytes 4194336 | tf_op jit(solution)/shard_map/all_to_all | solution.py:33
  76.3 9.3 %convolution_convert_fusion.1 = bf16[1024,1024]{1,0:T(8,128)(2,1)} fusion(bf16[1024,2048]{1,0:T(8,128)(2,1)} %bitcast.102, bf16[2048,1024]{1,0:T(8,128)(2,1)} %bitcast.8), kind=kOutput, calls=%fused_computation.42 | convolution fusion | flops 4296015872 | bytes 10485760 | tf_op jit(solution)/shard_map/dot_general | solution.py:38
  85.6 6.5 %reshape.200 = bf16[2,512,16,64]{3,2,1,0:T(8,128)(2,1)} reshape(bf16[1024,1024]{1,0:T(8,128)(2,1)} %convolution_convert_fusion.1) | data formatting | bytes 4194304 | tf_op jit(solution)/shard_map/reshape | solution.py:41
  92.1 5.6 copy.31
  97.7 9.2 %all-gather.7.cloned.1.call-done = bf16[2048,1024]{1,0:T(8,128)(2,1)} async-done(((bf16[16,1024]{1,0:T(8,128)(2,1)}), bf16[2048,1024]{1,0:T(8,128)(2,1)}) %all-gather.7.cloned.1.call-update) | async-done | bytes 4194320 | tf_op jit(solution)/shard_map/all_gather | solution.py:36
  106.8 9.3 %convolution_convert_fusion.2 = bf16[1024,1024]{1,0:T(8,128)(2,1)} fusion(bf16[1024,2048]{1,0:T(8,128)(2,1)} %fusion.43, bf16[2048,1024]{1,0:T(8,128)(2,1)} %all-gather.7.cloned.1.call-done), kind=kOutput, calls=%fused_computation.43 | convolution fusion | flops 4296015872 | bytes 10485760 | tf_op jit(solution)/shard_map/dot_general | solution.py:40
  116.1 6.4 %reshape.199 = bf16[2,512,16,64]{3,2,1,0:T(8,128)(2,1)} reshape(bf16[1024,1024]{1,0:T(8,128)(2,1)} %convolution_convert_fusion.2) | data formatting | bytes 4194304 | tf_op jit(solution)/shard_map/reshape | solution.py:43
  122.5 5.5 copy.30
  128.0 46.0 %all-gather.9.cloned.1.call-done = bf16[2048,1024]{1,0:T(8,128)(2,1)} async-done(((bf16[16,1024]{1,0:T(8,128)(2,1)}), bf16[2048,1024]{1,0:T(8,128)(2,1)}) %all-gather.9.cloned.1.call-update) | async-done | bytes 4194320 | tf_op jit(solution)/shard_map/all_gather | solution.py:35
  174.0 9.3 %convolution_convert_fusion = bf16[1024,1024]{1,0:T(8,128)(2,1)} fusion(bf16[1024,2048]{1,0:T(8,128)(2,1)} %fusion.43, bf16[2048,1024]{1,0:T(8,128)(2,1)} %all-gather.9.cloned.1.call-done), kind=kOutput, calls=%fused_computation.41 | convolution fusion | flops 4296015872 | bytes 10485760 | tf_op jit(solution)/shard_map/dot_general | solution.py:39
  183.3 6.4 reshape.201
  189.7 5.4 copy.32
  195.1 42.2 %while.10 = (s32[]{:T(128)}, bf16[2,512,16,64]{1,3,2,0:T(8,128)(2,1)}, bf16[2,512,16,64]{1,3,2,0:T(8,128)(2,1)}, s32[2]{0:T(128)S(1)}, bf16[2,512,16,64]{1,3,2,0...) while((s32[]{:T(128)}, bf16[2,512,16,64]{1,3,2,0:T(8,128)(2,1)}, ...), condition=%wide.region_4.5_spmd, body=%wide.region_1.4_spmd.sunk | while | flops 1095238656 | bytes 37817436 | solution.py:44
  195.1 0.6 dynamic_slice.62
  195.8 0.7 iota_compare_fusion.3
  196.5 10.8 %fusion.85 = (f32[16,512]{1,0:T(8,128)S(1)}, f32[16,512,512]{1,2,0:T(8,128)}) fusion(pred[512]{0:T(512)(128)(4,1)S(1)} %iota_compare_fusion.3, bf16[2,512,16,64]{1,3,2,0:T(8,128)(2,1)} %get-tuple-element.136, s32[]{:T(128)} %get-tuple-element.124, bf16[2,512,16,64]{1,3,2,0:T(8,128)(2,1)} %get-tuple-element.135), kind=kOutput, calls=%fused_computation.82.clone.1 | convolution fusion | flops 549454336 | bytes 18908672 | tf_op jit(solution)/shard_map/while/body/eval_jaxpr/sub | solution.py:15
  207.2 8.8 %fusion.86 = bf16[2,512,16,64]{1,3,2,0:T(8,128)(2,1)} fusion(bf16[2,512,16,64]{1,3,2,0:T(8,128)(2,1)} %get-tuple-element.125, s32[]{:T(128)} %get-tuple-element.124, f32[16,512,512]{1,2,0:T(8,128)} %get-tuple-element.115, f32[16,512]{1,0:T(8,128)S(1)} %get-tuple-element.116, bf16[2,512,16,64]{1,3,2,0:T(8,128)(2,1)} %get-tuple-element.133), kind=kOutput, calls=%fused_computation.14.clone.1 | convolution fusion | flops 545783808 | bytes 18908160 | tf_op jit(solution)/shard_map/while/body/eval_jaxpr/hqk,khd->qhd/dot_general | solution.py:16
  216.0 0.6 dynamic_slice.62
  216.7 0.7 iota_compare_fusion.3
  217.3 10.8 %fusion.85 = (f32[16,512]{1,0:T(8,128)S(1)}, f32[16,512,512]{1,2,0:T(8,128)}) fusion(pred[512]{0:T(512)(128)(4,1)S(1)} %iota_compare_fusion.3, bf16[2,512,16,64]{1,3,2,0:T(8,128)(2,1)} %get-tuple-element.136, s32[]{:T(128)} %get-tuple-element.124, bf16[2,512,16,64]{1,3,2,0:T(8,128)(2,1)} %get-tuple-element.135), kind=kOutput, calls=%fused_computation.82.clone.1 | convolution fusion | flops 549454336 | bytes 18908672 | tf_op jit(solution)/shard_map/while/body/eval_jaxpr/sub | solution.py:15
  228.1 9.2 %fusion.86 = bf16[2,512,16,64]{1,3,2,0:T(8,128)(2,1)} fusion(bf16[2,512,16,64]{1,3,2,0:T(8,128)(2,1)} %get-tuple-element.125, s32[]{:T(128)} %get-tuple-element.124, f32[16,512,512]{1,2,0:T(8,128)} %get-tuple-element.115, f32[16,512]{1,0:T(8,128)S(1)} %get-tuple-element.116, bf16[2,512,16,64]{1,3,2,0:T(8,128)(2,1)} %get-tuple-element.133), kind=kOutput, calls=%fused_computation.14.clone.1 | convolution fusion | flops 545783808 | bytes 18908160 | tf_op jit(solution)/shard_map/while/body/eval_jaxpr/hqk,khd->qhd/dot_general | solution.py:16
  237.3 3.8 copy.33
  241.1 1.9 copy.42
  243.1 0.0 copy-start.7
  243.1 9.2 %select_reduce_fusion.1 = f32[2,2048]{1,0:T(2,128)S(1)} fusion(pred[2,512]{1,0:T(4,128)(4,1)S(1)} %copy-done.4, bf16[1024,1024]{0,1:T(8,128)(2,1)} %bitcast.103, bf16[1024,2048]{1,0:T(8,128)(2,1)} %all-gather.11.cloned.1.call-done, bf16[2,512,2048]{2,1,0:T(8,128)(2,1)} %param.12), kind=kOutput, calls=%fused_computation.40 | convolution fusion | flops 4303351808 | bytes 10503168 | tf_op jit(solution)/shard_map/dot_general | solution.py:47
  252.3 0.2 multiply_reduce_fusion
  252.6 0.7 fusion.55
  253.2 0.0 all-gather.13.cloned.1.call-update
  253.3 0.0 all-reduce.4.cloned.1.call-start
  253.3 0.0 copy-done.2
  253.3 0.1 copy.26
  253.5 0.2 dynamic-update-slice
  253.7 63.0 %all-reduce = s32[256]{0:T(256)S(1)} all-reduce(s32[256]{0:T(256)S(1)} %dynamic-update-slice), channel_id=1, replica_groups=mesh['dp'=128] {'dp'}, use_global_device_ids=true, to_apply=%add | all-reduce | flops 256 | bytes 2048
  316.7 0.7 gather_fusion
  317.4 0.1 fusion.51
  317.6 0.1 reshape.185
  317.7 3.2 sort.17
  320.9 0.1 compare_select_fusion.3
  320.9 2.3 reshape.196
  323.2 2.0 fusion.66
  325.2 129.5 %gather_fusion.2 = f32[16384]{0:T(1024)S(1)} fusion(f32[256,512]{1,0:T(8,128)S(1)} %fusion.66, s32[16384]{0:T(1024)S(1)} %reshape.185), kind=kCustom, calls=%fused_computation.2 | custom fusion | bytes 262144 | tf_op jit(solution)/shard_map/jit(take_along_axis)/gather | solution.py:71
  454.7 0.1 reshape.188
  454.7 0.8 select_select_fusion
  455.5 0.0 all-reduce.4.cloned.1.call-update
  455.6 139.4 %all-reduce.4.cloned.1.call-done = f32[256,64]{1,0:T(8,128)} async-done(((f32[256,64]{1,0:T(8,128)}), f32[256,64]{1,0:T(8,128)}) %all-reduce.4.cloned.1.call-update) | async-done | bytes 65552
  595.0 0.7 dynamic-slice_bitcast_fusion
  595.7 33.8 %all-gather.1 = f32[128,2,64]{2,1,0:T(2,128)S(1)} all-gather(f32[1,2,64]{2,1,0:T(2,128)S(1)} %dynamic-slice_bitcast_fusion), channel_id=1, replica_groups=mesh['dp'=128] {'dp'}, dimensions={0}, use_global_device_ids=true | all-gather | bytes 66048 | tf_op jit(solution)/shard_map/all_gather | solution.py:75
  629.5 1.1 gather_fusion.1
  (23 shorter events, 0.1 us)
Async XLA Ops:
  6.5 316.7 %copy-start = (bf16[512,2048]{1,0:T(8,128)(2,1)S(1)}, bf16[512,2048]{1,0:T(8,128)(2,1)}, u32[]{:S(2)}) copy-start(bf16[512,2048]{1,0:T(8,128)(2,1)} %param.21) | copy-start | bytes 6291460
  6.5 100.3 %all-gather.7.cloned.1.call-start = ((), (), s32[]{:S(2)}) async-start(), calls=%async_computation.1 | async-start | bytes 4227072 | tf_op jit(solution)/shard_map/all_gather | solution.py:36
  7.3 166.8 %all-gather.9.cloned.1.call-start = ((), (), s32[]{:S(2)}) async-start(), calls=%async_computation.2 | async-start | bytes 4227072 | tf_op jit(solution)/shard_map/all_gather | solution.py:35
  11.3 65.0 %all-to-all-start = ((bf16[128,16,1024]{2,1,0:T(8,128)(2,1)}), bf16[128,16,1024]{2,1,0:T(8,128)(2,1)}, u32[]{:S(2)}, u32[]{:S(2)}) async-start(bf16[128,16,1024]{2,1,0:T(8,128)(2,1)} %stack.2), calls=%async_computation | async-start | bytes 8388608 | tf_op jit(solution)/shard_map/all_to_all | solution.py:33
  23.2 3.9 copy-start.6
  23.2 5.2 copy-start.3
  23.2 219.8 %all-gather.11.cloned.1.call-start = ((), (), s32[]{:S(2)}) async-start(), calls=%async_computation.3 | async-start | bytes 4227072 | tf_op jit(solution)/shard_map/all_gather | solution.py:48
  24.0 297.0 %all-gather.13.cloned.1.call-start = ((), (), s32[]{:S(2)}) async-start(), calls=%async_computation.4 | async-start | bytes 1056768 | tf_op jit(solution)/shard_map/all_gather | solution.py:64
  28.4 5.3 copy-start.1
  237.3 5.7 copy-start.4
  243.1 9.3 %copy-start.5 = (f32[2]{0:T(128)S(1)}, f32[2]{0:T(128)}, u32[]{:S(2)}) copy-start(f32[2]{0:T(128)} %convert_element_type.51) | copy-start | bytes 28
  243.1 10.3 %copy-start.2 = (s32[256,64]{0,1:T(8,128)S(1)}, s32[256,64]{0,1:T(8,128)}, u32[]{:S(2)}) copy-start(s32[256,64]{0,1:T(8,128)} %param.15) | copy-start | bytes 196612
  243.1 10.4 %copy-start.7 = (s32[2]{0:T(128)S(1)}, s32[2]{0:T(128)}, u32[]{:S(2)}) copy-start(s32[2]{0:T(128)} %param.14) | copy-start | bytes 28
  253.3 341.7 %all-reduce.4.cloned.1.call-start = ((), (), s32[]{:S(2)}) async-start(), calls=%async_computation.5 | async-start | bytes 262144
Sparse Core Ops, SparseCore 0:
  10.5 96.3 all-gather.6
  110.0 64.0 all-gather.8
  177.2 64.1 all-gather.10
  253.4 61.1 all-gather.12
  455.7 139.2 all-reduce.3
